TPU v7x, 256 devices: a whole 4x4x8 slice. The times are simulated.
256 devices in a mesh: section: 4 (over x), tm: 64 (over y, z, core).
Axes of the slice: x: 4, y: 4, z: 8, core: 2. Of those that a mesh axis runs over, the one named last changes fastest.
Arguments:
- signal: bfloat16 [4, 32768, 256], P(None, 'tm'), may hold values from -6 to 6
- skip_cot: bfloat16 [4, 32768, 256], P(None, 'tm'), may hold values from -6 to 6
- res_cot: bfloat16 [4, 32768, 256], P(None, 'tm'), may hold values from -6 to 6
- w_tap: bfloat16 [4, 256, 512], P('section'), may hold values from -0.25 to 0.25
- w_now: bfloat16 [4, 256, 512], P('section'), may hold values from -0.25 to 0.25
- w_res: bfloat16 [4, 256, 256], P('section'), may hold values from -0.375 to 0.375
- w_skip: bfloat16 [4, 256, 256], P('section'), may hold values from -0.375 to 0.375
Outputs:
- skip_total: bfloat16 [4, 32768, 256], P(None, 'tm')
- input_grads: bfloat16 [4, 4, 32768, 256], P('section', None, 'tm')
- grad_tap: float32 [4, 256, 512], P('section')
- grad_now: float32 [4, 256, 512], P('section')
- grad_res: float32 [4, 256, 256], P('section')
- grad_skip: float32 [4, 256, 256], P('section')
All inputs are finite; a program needn't handle non-finite values.
Results may differ from a plain program's by a relative error of at most 0.01.
Values may be sent and summed in bfloat16 or wider, within the bound.
A program may use at most 64 MiB of HBM per device.

v0:
```python
import math
import jax
import jax.numpy as jnp
from jax import lax
from jax.sharding import PartitionSpec as P

SPAN = 4


def passed_along(x, axis, by):
    size = lax.axis_size(axis)
    pairs = [(i, i + by) for i in range(size) if 0 <= i + by < size]
    return lax.ppermute(x, axis, pairs)


def flat_dot(left, right):
    result = jnp.dot(left.reshape(-1, left.shape[-1]), right, preferred_element_type=jnp.float32)
    return result.reshape(left.shape[:-1] + (right.shape[-1],))


def rows_spanning(left, right):
    return lax.dot_general(
        left.reshape(-1, left.shape[-1]),
        right.reshape(-1, right.shape[-1]),
        (((0,), (0,)), ((), ())),
        preferred_element_type=jnp.float32,
    )


def tap_rows(values, chosen, delayed):
    result = jnp.zeros_like(values)
    for layer_number, selected in chosen:
        if delayed:
            arrived = passed_along(values, "tm", SPAN << layer_number)
        else:
            arrived = passed_along(values, "tm", -(SPAN << layer_number))
        result = jnp.where(selected, arrived, result)
    return result


def gate_parts(tapped, layer_in, weights):
    pre = flat_dot(tapped, weights[0]) + flat_dot(layer_in, weights[1])
    half_width = pre.shape[-1] // 2
    return (jnp.tanh(pre[..., :half_width]), jax.nn.sigmoid(pre[..., half_width:]))


def layer_forward(layer_in, weights, chosen):
    tapped = tap_rows(layer_in, chosen, True)
    tanh_part, sigmoid_part = gate_parts(tapped, layer_in, weights)
    gated = (tanh_part * sigmoid_part).astype(jnp.bfloat16)
    stream_out = (layer_in.astype(jnp.float32) + flat_dot(gated, weights[2])).astype(jnp.bfloat16)
    return (tapped, stream_out, flat_dot(gated, weights[3]))


def layer_backward(layer_in, tapped, grad_out, skip_grad, weights, chosen):
    tanh_part, sigmoid_part = gate_parts(tapped, layer_in, weights)
    gated = (tanh_part * sigmoid_part).astype(jnp.bfloat16)
    grad_gated = flat_dot(grad_out, weights[2].T) + flat_dot(skip_grad, weights[3].T)
    grad_pre = jnp.concatenate(
        [
            grad_gated * sigmoid_part * (1.0 - tanh_part * tanh_part),
            grad_gated * tanh_part * sigmoid_part * (1.0 - sigmoid_part),
        ],
        axis=-1,
    ).astype(jnp.bfloat16)
    terms = (
        rows_spanning(tapped, grad_pre),
        rows_spanning(layer_in, grad_pre),
        rows_spanning(gated, grad_out),
        rows_spanning(gated, skip_grad),
    )
    back_term = flat_dot(grad_pre, weights[0].T).astype(jnp.bfloat16)
    arrived = tap_rows(back_term, chosen, False)
    grad_in = (
        grad_out.astype(jnp.float32)
        + flat_dot(grad_pre, weights[1].T)
        + arrived.astype(jnp.float32)
    )
    return (grad_in.astype(jnp.bfloat16), terms)


def run_sequences(signal, skip_cot, res_cot, w_tap, w_now, w_res, w_skip, section_index, sections):
    number = signal.shape[0]
    per_section = number // sections
    every_tap, every_now, every_res, skip_outputs_all = (
        lax.all_gather(w_tap, "section", axis=0, tiled=True),
        lax.all_gather(w_now, "section", axis=0, tiled=True),
        lax.all_gather(w_res, "section", axis=0, tiled=True),
        lax.all_gather(w_skip, "section", axis=0, tiled=True),
    )
    anchor = section_index * per_section
    stream = lax.dynamic_slice_in_dim(signal, anchor, per_section, 0)
    skip_grad = lax.dynamic_slice_in_dim(skip_cot, anchor, per_section, 0)
    grad_out = lax.dynamic_slice_in_dim(res_cot, anchor, per_section, 0)
    skip_running_sum = jnp.zeros(skip_grad.shape, jnp.float32)
    saved_in = []
    saved_tap = []
    for layer_number in range(sections):
        weights = (
            every_tap[layer_number],
            every_now[layer_number],
            every_res[layer_number],
            skip_outputs_all[layer_number],
        )
        tapped, stream_out, skip_term = layer_forward(stream, weights, [(layer_number, True)])
        saved_in.append(stream)
        saved_tap.append(tapped)
        skip_running_sum = skip_running_sum + skip_term
        stream = stream_out
    skip_total = lax.all_gather(
        skip_running_sum.astype(jnp.bfloat16), "section", axis=0, tiled=True
    )
    grad_list = [None] * sections
    term_list = [None] * sections
    for layer_number in reversed(range(sections)):
        weights = (
            every_tap[layer_number],
            every_now[layer_number],
            every_res[layer_number],
            skip_outputs_all[layer_number],
        )
        grad_in, terms = layer_backward(
            saved_in[layer_number],
            saved_tap[layer_number],
            grad_out,
            skip_grad,
            weights,
            [(layer_number, True)],
        )
        grad_list[layer_number] = grad_in
        term_list[layer_number] = terms
        grad_out = grad_in
    stacked = jnp.stack(grad_list)
    input_grads = lax.all_to_all(stacked, "section", split_axis=0, concat_axis=1, tiled=True)[0]
    partial_sums = (
        lax.psum_scatter(
            jnp.stack([term[0] for term in term_list]), "section", scatter_dimension=0, tiled=True
        ),
        lax.psum_scatter(
            jnp.stack([term[1] for term in term_list]), "section", scatter_dimension=0, tiled=True
        ),
        lax.psum_scatter(
            jnp.stack([term[2] for term in term_list]), "section", scatter_dimension=0, tiled=True
        ),
        lax.psum_scatter(
            jnp.stack([term[3] for term in term_list]), "section", scatter_dimension=0, tiled=True
        ),
    )
    return (skip_total, input_grads, tuple(partial_sums))


def body(signal, skip_cot, res_cot, w_tap, w_now, w_res, w_skip):
    sections = lax.axis_size("section")
    shards = lax.axis_size("tm")
    section_index = lax.axis_index("section")
    number, seq_rows, channels = signal.shape
    skip_total, input_grads, partial_sums = run_sequences(
        signal, skip_cot, res_cot, w_tap, w_now, w_res, w_skip, section_index, sections
    )
    summed = lax.psum((partial_sums[0], partial_sums[1], partial_sums[2], partial_sums[3]), "tm")
    grad_scale = 1.0 / math.sqrt(number * seq_rows * shards)
    return (
        skip_total,
        input_grads[None],
        summed[0] * grad_scale,
        summed[1] * grad_scale,
        summed[2] * grad_scale,
        summed[3] * grad_scale,
    )


def solution(mesh):
    in_specs = (
        P(None, "tm", None),
        P(None, "tm", None),
        P(None, "tm", None),
        P("section", None, None),
        P("section", None, None),
        P("section", None, None),
        P("section", None, None),
    )
    out_specs = (
        P(None, "tm", None),
        P("section", None, "tm", None),
        P("section", None, None),
        P("section", None, None),
        P("section", None, None),
        P("section", None, None),
    )
    return jax.shard_map(body, mesh=mesh, in_specs=in_specs, out_specs=out_specs, check_vma=False)
```

profile of v0, /device:TPU:2, one launch (start us, length us, event | category | flops | bytes accessed | tf_op | source)
XLA Modules:
  0.0 490.8 jit_solution(7062506059764534918)
XLA Ops:
  9.7 5.2 %collective-permute-start = (bf16[1,512,256]{2,1,0:T(8,128)(2,1)S(1)}, bf16[1,512,256]{2,1,0:T(8,128)(2,1)S(1)}, u32[]{:S(2)}, u32[]{:S(2)}) collective-permute-start(bf16[1,512,256]{2,1,0:T(8,128)(2,1)S(1)} %constant_dynamic-slice_fusion), channel_id=1, source_target_pairs={{0,4},{1,5},{2,6},{3,7},{4,8},{5,9},{6,10},{7,11},{8,12},{9,13},{1... | collective-permute-start | bytes 786440 | tf_op jit(solution)/shard_map/ppermute | solution.py:13
  14.9 14.2 %all_gather.18 = bf16[4,256,256]{2,1,0:T(8,128)(2,1)S(1)} all-gather(bf16[1,256,256]{2,1,0:T(8,128)(2,1)} %param.12), channel_id=1, replica_groups=mesh['section'=4,'tm'=64] {'section'}, dimensions={0}, use_global_device_ids=true | all-gather | bytes 655360 | tf_op jit(solution)/shard_map/all_gather | solution.py:88
  29.1 15.1 %all_gather.17 = bf16[4,256,256]{2,1,0:T(8,128)(2,1)S(1)} all-gather(bf16[1,256,256]{2,1,0:T(8,128)(2,1)} %param.13), channel_id=1, replica_groups=mesh['section'=4,'tm'=64] {'section'}, dimensions={0}, use_global_device_ids=true | all-gather | bytes 655360 | tf_op jit(solution)/shard_map/all_gather | solution.py:89
  44.3 2.2 fusion.63
  46.4 1.1 fusion.59
  47.5 1.3 fusion.81
  48.8 19.7 %all-gather.5.cloned.1.call-done = bf16[4,256,512]{2,1,0:T(8,128)(2,1)} async-done(((bf16[1,256,512]{2,1,0:T(8,128)(2,1)}), bf16[4,256,512]{2,1,0:T(8,128)(2,1)}) %all-gather.5.cloned.1.call-update) | async-done | bytes 1048592 | tf_op jit(solution)/shard_map/all_gather | solution.py:86
  68.5 1.3 fusion.3
  70.5 7.8 %collective-permute-start.1 = (bf16[1,512,256]{2,1,0:T(8,128)(2,1)S(1)}, bf16[1,512,256]{2,1,0:T(8,128)(2,1)S(1)}, u32[]{:S(2)}, u32[]{:S(2)}) collective-permute-start(bf16[1,512,256]{2,1,0:T(8,128)(2,1)S(1)} %fusion.14), channel_id=1, source_target_pairs={{0,8},{1,9},{2,10},{3,11},{4,12},{5,13},{6,14},{7,15},{8,16},{9,17... | collective-permute-start | bytes 786440 | tf_op jit(solution)/shard_map/ppermute | solution.py:13
  78.7 5.4 %collective-permute-done.1 = bf16[1,512,256]{2,1,0:T(8,128)(2,1)S(1)} collective-permute-done((bf16[1,512,256]{2,1,0:T(8,128)(2,1)S(1)}, bf16[1,512,256]{2,1,0:T(8,128)(2,1)S(1)}, u32[]{:S(2)}, u32[]{:S(2)}) %collective-permute-start.1) | collective-permute-done | bytes 262176 | tf_op jit(solution)/shard_map/ppermute | solution.py:13
  84.7 1.3 fusion.13
  86.3 5.7 %collective-permute-start.2 = (bf16[1,512,256]{2,1,0:T(8,128)(2,1)S(1)}, bf16[1,512,256]{2,1,0:T(8,128)(2,1)}, u32[]{:S(2)}, u32[]{:S(2)}) collective-permute-start(bf16[1,512,256]{2,1,0:T(8,128)(2,1)S(1)} %fusion.13), channel_id=1, source_target_pairs={{0,16},{1,17},{2,18},{3,19},{4,20},{5,21},{6,22},{7,23},{8,24},{9,... | collective-permute-start | bytes 786440 | tf_op jit(solution)/shard_map/ppermute | solution.py:13
  92.3 2.8 collective-permute-done.2
  95.1 1.3 fusion.1
  96.6 1.3 fusion.12
  98.2 6.2 %collective-permute-start.3 = (bf16[1,512,256]{2,1,0:T(8,128)(2,1)S(1)}, bf16[1,512,256]{2,1,0:T(8,128)(2,1)S(1)}, u32[]{:S(2)}, u32[]{:S(2)}) collective-permute-start(bf16[1,512,256]{2,1,0:T(8,128)(2,1)S(1)} %fusion.12), channel_id=1, source_target_pairs={{0,32},{1,33},{2,34},{3,35},{4,36},{5,37},{6,38},{7,39},{8,40},{9,... | collective-permute-start | bytes 786440 | tf_op jit(solution)/shard_map/ppermute | solution.py:13
  104.7 3.5 collective-permute-done.3
  109.1 1.1 fusion.16
  110.2 1.3 collective-permute-start.4
  111.7 1.1 pad_maximum_fusion.4
  112.9 7.4 %collective-permute-done.4 = bf16[1,512,256]{2,1,0:T(8,128)(2,1)} collective-permute-done((bf16[1,512,256]{2,1,0:T(8,128)(2,1)}, bf16[1,512,256]{2,1,0:T(8,128)(2,1)}, u32[]{:S(2)}, u32[]{:S(2)}) %collective-permute-start.4) | collective-permute-done | bytes 262176 | tf_op jit(solution)/shard_map/ppermute | solution.py:13
  120.3 1.6 add_convert_fusion.3
  121.9 1.9 fusion.38
  124.2 1.4 collective-permute-start.5
  126.0 1.2 convolution_bitcast_fusion.19
  127.2 5.5 %collective-permute-done.5 = bf16[1,512,256]{2,1,0:T(8,128)(2,1)S(1)} collective-permute-done((bf16[1,512,256]{2,1,0:T(8,128)(2,1)S(1)}, bf16[1,512,256]{2,1,0:T(8,128)(2,1)S(1)}, u32[]{:S(2)}, u32[]{:S(2)}) %collective-permute-start.5) | collective-permute-done | bytes 262176 | tf_op jit(solution)/shard_map/ppermute | solution.py:13
  133.0 1.4 fusion.40
  134.9 1.3 collective-permute-start.6
  136.6 10.4 %collective-permute-done.6 = bf16[1,512,256]{2,1,0:T(8,128)(2,1)S(1)} collective-permute-done((bf16[1,512,256]{2,1,0:T(8,128)(2,1)S(1)}, bf16[1,512,256]{2,1,0:T(8,128)(2,1)S(1)}, u32[]{:S(2)}, u32[]{:S(2)}) %collective-permute-start.6) | collective-permute-done | bytes 262176 | tf_op jit(solution)/shard_map/ppermute | solution.py:13
  149.6 1.5 convolution_bitcast_fusion
  151.8 1.3 fusion.42
  154.3 1.5 pad_maximum_fusion.1
  156.1 1.5 convolution_bitcast_fusion.4
  157.6 1.5 convolution_bitcast_fusion.5
  159.1 1.4 convolution_bitcast_fusion.6
  160.9 1.5 pad_maximum_fusion
  164.4 1.4 fusion.19
  165.8 1.3 collective-permute-start.7
  167.1 14.1 %collective-permute-done.7 = bf16[1,512,256]{2,1,0:T(8,128)(2,1)S(1)} collective-permute-done((bf16[1,512,256]{2,1,0:T(8,128)(2,1)S(1)}, bf16[1,512,256]{2,1,0:T(8,128)(2,1)S(1)}, u32[]{:S(2)}, u32[]{:S(2)}) %collective-permute-start.7) | collective-permute-done | bytes 262176 | tf_op jit(solution)/shard_map/ppermute | solution.py:13
  181.2 1.4 fusion.44
  182.6 1.1 pad_maximum_fusion.2
  183.7 6.6 %all-to-all-start = ((bf16[4,1,512,256]{3,2,1,0:T(8,128)(2,1)}), bf16[4,1,512,256]{3,2,1,0:T(8,128)(2,1)S(1)}, u32[]{:S(2)}, u32[]{:S(2)}) async-start(bf16[4,1,512,256]{3,2,1,0:T(8,128)(2,1)} %pad_maximum_fusion.2), calls=%async_computation | async-start | bytes 2097152 | tf_op jit(solution)/shard_map/all_to_all | solution.py:134
  190.3 27.4 %reduce-scatter.7.cloned.1.call-done = f32[1,256,512]{2,1,0:T(8,128)} async-done(((f32[4,256,512]{2,1,0:T(8,128)}), f32[1,256,512]{2,1,0:T(8,128)}) %reduce-scatter.7.cloned.1.call-update) | async-done | bytes 524304 | tf_op jit(solution)/shard_map/reduce_scatter | solution.py:139
  217.7 36.6 %reduce-scatter.5.cloned.1.call-done = f32[1,256,512]{2,1,0:T(8,128)} async-done(((f32[4,256,512]{2,1,0:T(8,128)}), f32[1,256,512]{2,1,0:T(8,128)}) %reduce-scatter.5.cloned.1.call-update) | async-done | bytes 524304 | tf_op jit(solution)/shard_map/reduce_scatter | solution.py:136
  254.4 28.9 %all-gather.9.cloned.1.call-done = bf16[2048,256]{1,0:T(8,128)(2,1)} async-done(((bf16[512,256]{1,0:T(8,128)(2,1)}), bf16[2048,256]{1,0:T(8,128)(2,1)}) %all-gather.9.cloned.1.call-update) | async-done | bytes 1048592 | tf_op jit(solution)/shard_map/all_gather | solution.py:110
  283.2 194.7 %all-reduce.3.cloned.1.call-done = (f32[1,256,512]{2,1,0:T(8,128)}, f32[1,256,512]{2,1,0:T(8,128)}, f32[1,256,256]{2,1,0:T(8,128)}, f32[1,256,256]{2,1,0:T(8,128)}) async-done(((f32[1,256,512]{2,1,0:T(8,128)}, f32[1,256,512]{2,1,0:T(8,128)}, f32[1,256,256]{2,1,0:T(8,128)}, f32[1,256,256]{2,1,0:T(8,128)}), (f32[1,256,512]{2,1,0:T(8,128)}, f32[1,256,512]{2,1,0:T(8,128)}, f32[1,256,256]{2,1,0:T(8,128)}, ...) | async-done | bytes 1572880 | tf_op jit(solution)/shard_map/psum | solution.py:160
  477.9 1.9 broadcast_multiply_fusion.2
  479.8 2.3 broadcast_multiply_fusion
  (148 shorter events, 17.1 us)
Async XLA Ops:
  7.2 39.3 %copy-start = (bf16[4,512,256]{2,1,0:T(8,128)(2,1)S(1)}, bf16[4,512,256]{2,1,0:T(8,128)(2,1)}, u32[]{:S(2)}) copy-start(bf16[4,512,256]{2,1,0:T(8,128)(2,1)} %param.8) | copy-start | bytes 3145732
  7.2 40.3 %all-gather.7.cloned.1.call-start = ((), (), s32[]{:S(2)}) async-start(), calls=%async_computation.6 | async-start | bytes 1310720 | tf_op jit(solution)/shard_map/all_gather | solution.py:87
  7.9 60.6 %all-gather.5.cloned.1.call-start = ((), (), s32[]{:S(2)}) async-start(), calls=%async_computation.5 | async-start | bytes 1310720 | tf_op jit(solution)/shard_map/all_gather | solution.py:86
  8.7 181.6 %reduce-scatter.11.cloned.1.call-start = ((), (), s32[]{:S(2)}) async-start(), calls=%async_computation.10 | async-start | bytes 1310720 | tf_op jit(solution)/shard_map/reduce_scatter | solution.py:145
  9.7 39.1 %collective-permute-start = (bf16[1,512,256]{2,1,0:T(8,128)(2,1)S(1)}, bf16[1,512,256]{2,1,0:T(8,128)(2,1)S(1)}, u32[]{:S(2)}, u32[]{:S(2)}) collective-permute-start(bf16[1,512,256]{2,1,0:T(8,128)(2,1)S(1)} %constant_dynamic-slice_fusion), channel_id=1, source_target_pairs={{0,4},{1,5},{2,6},{3,7},{4,8},{5,9},{6,10},{7,11},{8,12},{9,13},{1... | collective-permute-start | bytes 786440 | tf_op jit(solution)/shard_map/ppermute | solution.py:13
  29.1 55.0 %copy-start.11 = (bf16[4,256,256]{2,1,0:T(8,128)(2,1)}, bf16[4,256,256]{2,1,0:T(8,128)(2,1)S(1)}, u32[]{:S(2)}) copy-start(bf16[4,256,256]{2,1,0:T(8,128)(2,1)S(1)} %all_gather.18) | copy-start | bytes 1572868
  48.8 19.7 %copy-start.14 = (bf16[1,512,256]{2,1,0:T(8,128)(2,1)}, bf16[1,512,256]{2,1,0:T(8,128)(2,1)S(1)}, u32[]{:S(2)}) copy-start(bf16[1,512,256]{2,1,0:T(8,128)(2,1)S(1)} %collective-permute-done) | copy-start | bytes 786436
  69.8 8.9 %copy-start.1 = (f32[1,512,512]{1,2,0:T(8,128)}, f32[1,512,512]{1,2,0:T(8,128)S(1)}, u32[]{:S(2)}) copy-start(f32[1,512,512]{1,2,0:T(8,128)S(1)} %fusion.3) | copy-start | bytes 3145732
  69.8 8.6 %copy-start.36 = (bf16[4,256,512]{2,1,0:T(8,128)(2,1)S(1)}, bf16[4,256,512]{2,1,0:T(8,128)(2,1)}, u32[]{:S(2)}) copy-start(bf16[4,256,512]{2,1,0:T(8,128)(2,1)} %all-gather.7.cloned.1.call-done) | copy-start | bytes 3145732
  69.8 14.3 %copy-start.12 = (bf16[4,256,512]{2,1,0:T(8,128)(2,1)S(1)}, bf16[4,256,512]{2,1,0:T(8,128)(2,1)}, u32[]{:S(2)}) copy-start(bf16[4,256,512]{2,1,0:T(8,128)(2,1)} %all-gather.5.cloned.1.call-done) | copy-start | bytes 3145732
  70.5 13.6 %collective-permute-start.1 = (bf16[1,512,256]{2,1,0:T(8,128)(2,1)S(1)}, bf16[1,512,256]{2,1,0:T(8,128)(2,1)S(1)}, u32[]{:S(2)}, u32[]{:S(2)}) collective-permute-start(bf16[1,512,256]{2,1,0:T(8,128)(2,1)S(1)} %fusion.14), channel_id=1, source_target_pairs={{0,8},{1,9},{2,10},{3,11},{4,12},{5,13},{6,14},{7,15},{8,16},{9,17... | collective-permute-start | bytes 786440 | tf_op jit(solution)/shard_map/ppermute | solution.py:13
  84.5 7.8 %copy-start.3 = (f32[1,512,512]{1,2,0:T(8,128)}, f32[1,512,512]{1,2,0:T(8,128)S(1)}, u32[]{:S(2)}) copy-start(f32[1,512,512]{1,2,0:T(8,128)S(1)} %fusion.2) | copy-start | bytes 3145732
  86.3 8.8 %collective-permute-start.2 = (bf16[1,512,256]{2,1,0:T(8,128)(2,1)S(1)}, bf16[1,512,256]{2,1,0:T(8,128)(2,1)}, u32[]{:S(2)}, u32[]{:S(2)}) collective-permute-start(bf16[1,512,256]{2,1,0:T(8,128)(2,1)S(1)} %fusion.13), channel_id=1, source_target_pairs={{0,16},{1,17},{2,18},{3,19},{4,20},{5,21},{6,22},{7,23},{8,24},{9,... | collective-permute-start | bytes 786440 | tf_op jit(solution)/shard_map/ppermute | solution.py:13
  96.4 8.3 %copy-start.5 = (f32[1,512,512]{1,2,0:T(8,128)}, f32[1,512,512]{1,2,0:T(8,128)S(1)}, u32[]{:S(2)}) copy-start(f32[1,512,512]{1,2,0:T(8,128)S(1)} %fusion.1) | copy-start | bytes 3145732
  98.2 10.4 %copy-start.7 = (bf16[4,256,256]{2,1,0:T(8,128)(2,1)S(1)}, bf16[4,256,256]{2,1,0:T(8,128)(2,1)}, u32[]{:S(2)}) copy-start(bf16[4,256,256]{2,1,0:T(8,128)(2,1)} %copy-done.6) | copy-start | bytes 1572868
  98.2 10.4 %copy-start.45 = (f32[512,256]{0,1:T(8,128)S(1)}, f32[512,256]{0,1:T(8,128)}, u32[]{:S(2)}) copy-start(f32[512,256]{0,1:T(8,128)} %fusion.63) | copy-start | bytes 1572868
  98.2 10.0 %collective-permute-start.3 = (bf16[1,512,256]{2,1,0:T(8,128)(2,1)S(1)}, bf16[1,512,256]{2,1,0:T(8,128)(2,1)S(1)}, u32[]{:S(2)}, u32[]{:S(2)}) collective-permute-start(bf16[1,512,256]{2,1,0:T(8,128)(2,1)S(1)} %fusion.12), channel_id=1, source_target_pairs={{0,32},{1,33},{2,34},{3,35},{4,36},{5,37},{6,38},{7,39},{8,40},{9,... | collective-permute-start | bytes 786440 | tf_op jit(solution)/shard_map/ppermute | solution.py:13
  109.1 2.4 copy-start.8
  109.1 2.6 copy-start.19
  109.1 2.6 copy-start.20
  110.2 10.1 %collective-permute-start.4 = (bf16[1,512,256]{2,1,0:T(8,128)(2,1)}, bf16[1,512,256]{2,1,0:T(8,128)(2,1)}, u32[]{:S(2)}, u32[]{:S(2)}) collective-permute-start(bf16[1,512,256]{2,1,0:T(8,128)(2,1)} %fusion.16), channel_id=1, source_target_pairs={{32,0},{33,1},{34,2},{35,3},{36,4},{37,5},{38,6},{39,7},{40,8},{41... | collective-permute-start | bytes 786440 | tf_op jit(solution)/shard_map/ppermute | solution.py:13
  112.8 77.5 %reduce-scatter.9.cloned.1.call-start = ((), (), s32[]{:S(2)}) async-start(), calls=%async_computation.9 | async-start | bytes 1310720 | tf_op jit(solution)/shard_map/reduce_scatter | solution.py:142
  121.9 14.3 %copy-start.38 = (bf16[1,512,256]{2,1,0:T(8,128)(2,1)}, bf16[1,512,256]{2,1,0:T(8,128)(2,1)S(1)}, u32[]{:S(2)}) copy-start(bf16[1,512,256]{2,1,0:T(8,128)(2,1)S(1)} %add_convert_fusion.3) | copy-start | bytes 786436
  123.8 9.2 %copy-start.21 = (bf16[512,256]{0,1:T(8,128)(2,1)}, bf16[512,256]{0,1:T(8,128)(2,1)S(1)}, u32[]{:S(2)}) copy-start(bf16[512,256]{0,1:T(8,128)(2,1)S(1)} %get-tuple-element.14) | copy-start | bytes 786436
  123.8 9.2 %copy-start.23 = (bf16[512,256]{0,1:T(8,128)(2,1)}, bf16[512,256]{0,1:T(8,128)(2,1)S(1)}, u32[]{:S(2)}) copy-start(bf16[512,256]{0,1:T(8,128)(2,1)S(1)} %get-tuple-element.15) | copy-start | bytes 786436
  123.9 8.8 %copy-start.37 = (bf16[4,256,512]{2,1,0:T(8,128)(2,1)S(1)}, bf16[4,256,512]{2,1,0:T(8,128)(2,1)}, u32[]{:S(2)}) copy-start(bf16[4,256,512]{2,1,0:T(8,128)(2,1)} %all-gather.7.cloned.1.call-done) | copy-start | bytes 3145732
  124.2 8.8 %copy-start.4 = (f32[1,512,512]{1,2,0:T(8,128)S(1)}, f32[1,512,512]{1,2,0:T(8,128)}, u32[]{:S(2)}) copy-start(f32[1,512,512]{1,2,0:T(8,128)} %copy-done.3) | copy-start | bytes 3145732
  124.2 8.4 %collective-permute-start.5 = (bf16[1,512,256]{2,1,0:T(8,128)(2,1)S(1)}, bf16[1,512,256]{2,1,0:T(8,128)(2,1)S(1)}, u32[]{:S(2)}, u32[]{:S(2)}) collective-permute-start(bf16[1,512,256]{2,1,0:T(8,128)(2,1)S(1)} %fusion.17), channel_id=1, source_target_pairs={{16,0},{17,1},{18,2},{19,3},{20,4},{21,5},{22,6},{23,7},{24,8},{25... | collective-permute-start | bytes 786440 | tf_op jit(solution)/shard_map/ppermute | solution.py:13
  133.0 14.0 %copy-start.40 = (bf16[1,512,256]{2,1,0:T(8,128)(2,1)}, bf16[1,512,256]{2,1,0:T(8,128)(2,1)S(1)}, u32[]{:S(2)}) copy-start(bf16[1,512,256]{2,1,0:T(8,128)(2,1)S(1)} %add_convert_fusion.2) | copy-start | bytes 786436
  134.5 12.9 %copy-start.31 = (bf16[512,256]{0,1:T(8,128)(2,1)}, bf16[512,256]{0,1:T(8,128)(2,1)S(1)}, u32[]{:S(2)}) copy-start(bf16[512,256]{0,1:T(8,128)(2,1)S(1)} %get-tuple-element.12) | copy-start | bytes 786436
  134.5 12.9 %copy-start.33 = (bf16[512,256]{0,1:T(8,128)(2,1)}, bf16[512,256]{0,1:T(8,128)(2,1)S(1)}, u32[]{:S(2)}) copy-start(bf16[512,256]{0,1:T(8,128)(2,1)S(1)} %get-tuple-element.13) | copy-start | bytes 786436
  134.9 12.2 %collective-permute-start.6 = (bf16[1,512,256]{2,1,0:T(8,128)(2,1)S(1)}, bf16[1,512,256]{2,1,0:T(8,128)(2,1)S(1)}, u32[]{:S(2)}, u32[]{:S(2)}) collective-permute-start(bf16[1,512,256]{2,1,0:T(8,128)(2,1)S(1)} %fusion.18), channel_id=1, source_target_pairs={{8,0},{9,1},{10,2},{11,3},{12,4},{13,5},{14,6},{15,7},{16,8},{17,9... | collective-permute-start | bytes 786440 | tf_op jit(solution)/shard_map/ppermute | solution.py:13
  149.2 68.5 %reduce-scatter.7.cloned.1.call-start = ((), (), s32[]{:S(2)}) async-start(), calls=%async_computation.8 | async-start | bytes 2621440 | tf_op jit(solution)/shard_map/reduce_scatter | solution.py:139
  149.6 2.3 copy-start.2
  149.6 2.3 copy-start.43
  155.8 3.3 copy-start.17
  155.9 4.6 copy-start.15
  155.9 98.5 %reduce-scatter.5.cloned.1.call-start = ((), (), s32[]{:S(2)}) async-start(), calls=%async_computation.7 | async-start | bytes 2621440 | tf_op jit(solution)/shard_map/reduce_scatter | solution.py:136
  156.1 4.4 copy-start.26
  156.1 4.4 copy-start.29
  162.5 120.8 %all-gather.9.cloned.1.call-start = ((), (), s32[]{:S(2)}) async-start(), calls=%async_computation.11 | async-start | bytes 1310720 | tf_op jit(solution)/shard_map/all_gather | solution.py:110
  164.4 18.2 %copy-start.39 = (bf16[1,512,256]{2,1,0:T(8,128)(2,1)S(1)}, bf16[1,512,256]{2,1,0:T(8,128)(2,1)}, u32[]{:S(2)}) copy-start(bf16[1,512,256]{2,1,0:T(8,128)(2,1)} %copy-done.38) | copy-start | bytes 786436
  164.4 18.2 %copy-start.41 = (bf16[1,512,256]{2,1,0:T(8,128)(2,1)S(1)}, bf16[1,512,256]{2,1,0:T(8,128)(2,1)}, u32[]{:S(2)}) copy-start(bf16[1,512,256]{2,1,0:T(8,128)(2,1)} %copy-done.40) | copy-start | bytes 786436
  164.4 18.2 %copy-start.44 = (bf16[1,512,256]{2,1,0:T(8,128)(2,1)S(1)}, bf16[1,512,256]{2,1,0:T(8,128)(2,1)}, u32[]{:S(2)}) copy-start(bf16[1,512,256]{2,1,0:T(8,128)(2,1)} %copy-done.42) | copy-start | bytes 786436
  165.8 15.4 %collective-permute-start.7 = (bf16[1,512,256]{2,1,0:T(8,128)(2,1)S(1)}, bf16[1,512,256]{2,1,0:T(8,128)(2,1)S(1)}, u32[]{:S(2)}, u32[]{:S(2)}) collective-permute-start(bf16[1,512,256]{2,1,0:T(8,128)(2,1)S(1)} %fusion.19), channel_id=1, source_target_pairs={{4,0},{5,1},{6,2},{7,3},{8,4},{9,5},{10,6},{11,7},{12,8},{13,9},{1... | collective-permute-start | bytes 786440 | tf_op jit(solution)/shard_map/ppermute | solution.py:13
  183.7 99.5 %all-to-all-start = ((bf16[4,1,512,256]{3,2,1,0:T(8,128)(2,1)}), bf16[4,1,512,256]{3,2,1,0:T(8,128)(2,1)S(1)}, u32[]{:S(2)}, u32[]{:S(2)}) async-start(bf16[4,1,512,256]{3,2,1,0:T(8,128)(2,1)} %pad_maximum_fusion.2), calls=%async_computation | async-start | bytes 2097152 | tf_op jit(solution)/shard_map/all_to_all | solution.py:134
  190.3 287.6 %all-reduce.3.cloned.1.call-start = ((), (), s32[]{:S(2)}) async-start(), calls=%async_computation.12 | async-start | bytes 3145728 | tf_op jit(solution)/shard_map/psum | solution.py:160
  283.2 198.8 %copy-start.35 = (bf16[2048,256]{1,0:T(8,128)(2,1)S(1)}, bf16[2048,256]{1,0:T(8,128)(2,1)}, u32[]{:S(2)}) copy-start(bf16[2048,256]{1,0:T(8,128)(2,1)} %all-gather.9.cloned.1.call-done) | copy-start | bytes 3145732
  (15 other events, 23.4 us)
Sparse Core Ops, SparseCore 0:
  9.8 30.3 all-gather.6
  42.0 26.4 all-gather.4
  113.0 31.7 reduce-scatter.10
  149.3 30.7 reduce-scatter.8
  182.5 35.1 reduce-scatter.6
  220.1 34.1 reduce-scatter.4
  256.7 26.4 all-gather.8
  286.9 190.9 all-reduce.2
where the time goes:
time: 492 us; the launch traced here: 491 us
  waiting for transfers between devices  358 us (73%)
  starting transfers between devices  37.1 us (8%)
  matrix products  35.9 us (7%)
  blocking collectives  29.4 us (6%)
  between operations  15.1 us (3%)
  other arithmetic  11.1 us (2%)
    psum x1, waiting for transfers between devices, body(): lax.psum((partial_sums[0], partial_sums[1], partial_sums[2], partial_sums...  195 us
    ppermute x8, waiting for transfers between devices, passed_along(): return lax.ppermute(x, axis, pairs)  49.1 us
    reduce_scatter x1, waiting for transfers between devices, run_sequences(): lax.psum_scatter(jnp.stack([term[0] for term in term_list]), 'section', s...  36.6 us
    ppermute x8, starting transfers between devices, passed_along(): return lax.ppermute(x, axis, pairs)  30.1 us
    all_gather x1, waiting for transfers between devices, run_sequences(): lax.all_gather(skip_running_sum.astype(jnp.bfloat16), 'section', axis=0,...  28.9 us
    reduce_scatter x1, waiting for transfers between devices, run_sequences(): lax.psum_scatter(jnp.stack([term[1] for term in term_list]), 'section', s...  27.4 us
    dot_general x31, matrix products, flat_dot(): jnp.dot(left.reshape(-1, left.shape[-1]), right, preferred_element_type=j...  25.9 us
    all_gather x1, waiting for transfers between devices, run_sequences(): lax.all_gather(w_tap, 'section', axis=0, tiled=True)  19.7 us
  transfers between devices with their start and end apart: 17, of which 12 were waited for; matrix products, arithmetic and copies ran while one was open for 7% of the time, Pallas kernels for 0%

commit v1 on v0

--- a/solution.py
+++ b/solution.py
@@ -107,8 +107,14 @@
         saved_tap.append(tapped)
         skip_running_sum = skip_running_sum + skip_term
         stream = stream_out
-    skip_total = lax.all_gather(
-        skip_running_sum.astype(jnp.bfloat16), "section", axis=0, tiled=True
+    skip_total = jnp.concatenate(
+        lax.all_to_all(
+            jnp.stack([skip_running_sum.astype(jnp.bfloat16)] * lax.axis_size("section")),
+            "section",
+            0,
+            0,
+        ),
+        axis=0,
     )
     grad_list = [None] * sections
     term_list = [None] * sections

time: 492 us -> 467 us (0.949)
  waiting for transfers between devices: 358 us -> 330 us
    all_gather x1 -> x0, waiting for transfers between devices: 28.9 us -> none  [run_sequences(): lax.all_gather(skip_running_sum.astype(jnp.bfloat16), 'section', axis=0,...]
    all_to_all x0 -> x1, starting transfers between devices: none -> 5.21 us  [run_sequences(): lax.all_to_all(jnp.stack([skip_running_sum.astype(jnp.bfloat16)] * lax.ax...]
  transfers between devices with their start and end apart: 17 -> 17, of which waited for: 12 -> 11; matrix products, arithmetic and copies ran while one was open for 7% -> 8% of each run, Pallas kernels for 0% -> 0%
where the time goes in v1:
time: 467 us; the launch traced here: 466 us
  waiting for transfers between devices  330 us (71%)
  starting transfers between devices  39.7 us (9%)
  matrix products  34.2 us (7%)
  blocking collectives  29.4 us (6%)
  between operations  15.1 us (3%)
  other arithmetic  11.2 us (2%)
  local copies, waits for them, and re-layouts  6.23 us (1%)
    psum x1, waiting for transfers between devices, body(): lax.psum((partial_sums[0], partial_sums[1], partial_sums[2], partial_sums...  194 us
    ppermute x8, waiting for transfers between devices, passed_along(): return lax.ppermute(x, axis, pairs)  52.6 us
    reduce_scatter x1, waiting for transfers between devices, run_sequences(): lax.psum_scatter(jnp.stack([term[0] for term in term_list]), 'section', s...  35.1 us
    ppermute x8, starting transfers between devices, passed_along(): return lax.ppermute(x, axis, pairs)  29.3 us
    reduce_scatter x1, waiting for transfers between devices, run_sequences(): lax.psum_scatter(jnp.stack([term[1] for term in term_list]), 'section', s...  26.8 us
    dot_general x31, matrix products, flat_dot(): jnp.dot(left.reshape(-1, left.shape[-1]), right, preferred_element_type=j...  24.2 us
    all_gather x1, waiting for transfers between devices, run_sequences(): lax.all_gather(w_tap, 'section', axis=0, tiled=True)  19.6 us
    all_gather x1, blocking collectives, run_sequences(): lax.all_gather(w_skip, 'section', axis=0, tiled=True)  15.1 us
  transfers between devices with their start and end apart: 17, of which 11 were waited for; matrix products, arithmetic and copies ran while one was open for 8% of the time, Pallas kernels for 0%

profile of v1, /device:TPU:2, one launch (start us, length us, event | category | flops | bytes accessed | tf_op | source)
XLA Modules:
  0.0 465.7 jit_solution(3592351414632953267)
XLA Ops:
  9.7 5.2 %collective-permute-start = (bf16[1,512,256]{2,1,0:T(8,128)(2,1)S(1)}, bf16[1,512,256]{2,1,0:T(8,128)(2,1)S(1)}, u32[]{:S(2)}, u32[]{:S(2)}) collective-permute-start(bf16[1,512,256]{2,1,0:T(8,128)(2,1)S(1)} %constant_dynamic-slice_fusion), channel_id=1, source_target_pairs={{0,4},{1,5},{2,6},{3,7},{4,8},{5,9},{6,10},{7,11},{8,12},{9,13},{1... | collective-permute-start | bytes 786440 | tf_op jit(solution)/shard_map/ppermute | solution.py:13
  14.9 14.2 %all_gather.15 = bf16[4,256,256]{2,1,0:T(8,128)(2,1)S(1)} all-gather(bf16[1,256,256]{2,1,0:T(8,128)(2,1)} %param.12), channel_id=1, replica_groups=mesh['section'=4,'tm'=64] {'section'}, dimensions={0}, use_global_device_ids=true | all-gather | bytes 655360 | tf_op jit(solution)/shard_map/all_gather | solution.py:88
  29.1 15.1 %all_gather.14 = bf16[4,256,256]{2,1,0:T(8,128)(2,1)S(1)} all-gather(bf16[1,256,256]{2,1,0:T(8,128)(2,1)} %param.13), channel_id=1, replica_groups=mesh['section'=4,'tm'=64] {'section'}, dimensions={0}, use_global_device_ids=true | all-gather | bytes 655360 | tf_op jit(solution)/shard_map/all_gather | solution.py:89
  44.3 2.2 fusion.63
  46.4 1.1 fusion.59
  47.5 1.3 fusion.81
  48.8 19.6 %all-gather.3.cloned.1.call-done = bf16[4,256,512]{2,1,0:T(8,128)(2,1)} async-done(((bf16[1,256,512]{2,1,0:T(8,128)(2,1)}), bf16[4,256,512]{2,1,0:T(8,128)(2,1)}) %all-gather.3.cloned.1.call-update) | async-done | bytes 1048592 | tf_op jit(solution)/shard_map/all_gather | solution.py:86
  68.5 1.3 fusion.3
  70.5 7.8 %collective-permute-start.1 = (bf16[1,512,256]{2,1,0:T(8,128)(2,1)S(1)}, bf16[1,512,256]{2,1,0:T(8,128)(2,1)S(1)}, u32[]{:S(2)}, u32[]{:S(2)}) collective-permute-start(bf16[1,512,256]{2,1,0:T(8,128)(2,1)S(1)} %fusion.14), channel_id=1, source_target_pairs={{0,8},{1,9},{2,10},{3,11},{4,12},{5,13},{6,14},{7,15},{8,16},{9,17... | collective-permute-start | bytes 786440 | tf_op jit(solution)/shard_map/ppermute | solution.py:13
  78.7 5.4 %collective-permute-done.1 = bf16[1,512,256]{2,1,0:T(8,128)(2,1)S(1)} collective-permute-done((bf16[1,512,256]{2,1,0:T(8,128)(2,1)S(1)}, bf16[1,512,256]{2,1,0:T(8,128)(2,1)S(1)}, u32[]{:S(2)}, u32[]{:S(2)}) %collective-permute-start.1) | collective-permute-done | bytes 262176 | tf_op jit(solution)/shard_map/ppermute | solution.py:13
  84.7 1.3 fusion.13
  86.3 4.9 %collective-permute-start.2 = (bf16[1,512,256]{2,1,0:T(8,128)(2,1)S(1)}, bf16[1,512,256]{2,1,0:T(8,128)(2,1)S(1)}, u32[]{:S(2)}, u32[]{:S(2)}) collective-permute-start(bf16[1,512,256]{2,1,0:T(8,128)(2,1)S(1)} %fusion.13), channel_id=1, source_target_pairs={{0,16},{1,17},{2,18},{3,19},{4,20},{5,21},{6,22},{7,23},{8,24},{9,... | collective-permute-start | bytes 786440 | tf_op jit(solution)/shard_map/ppermute | solution.py:13
  91.6 3.5 collective-permute-done.2
  96.4 1.3 fusion.12
  98.0 6.1 %collective-permute-start.3 = (bf16[1,512,256]{2,1,0:T(8,128)(2,1)S(1)}, bf16[1,512,256]{2,1,0:T(8,128)(2,1)S(1)}, u32[]{:S(2)}, u32[]{:S(2)}) collective-permute-start(bf16[1,512,256]{2,1,0:T(8,128)(2,1)S(1)} %fusion.12), channel_id=1, source_target_pairs={{0,32},{1,33},{2,34},{3,35},{4,36},{5,37},{6,38},{7,39},{8,40},{9,... | collective-permute-start | bytes 786440 | tf_op jit(solution)/shard_map/ppermute | solution.py:13
  104.4 3.5 collective-permute-done.3
  108.8 1.1 fusion.16
  109.8 1.3 collective-permute-start.4
  111.4 1.1 pad_maximum_fusion.4
  112.5 7.4 %collective-permute-done.4 = bf16[1,512,256]{2,1,0:T(8,128)(2,1)} collective-permute-done((bf16[1,512,256]{2,1,0:T(8,128)(2,1)}, bf16[1,512,256]{2,1,0:T(8,128)(2,1)}, u32[]{:S(2)}, u32[]{:S(2)}) %collective-permute-start.4) | collective-permute-done | bytes 262176 | tf_op jit(solution)/shard_map/ppermute | solution.py:13
  119.9 1.6 add_convert_fusion.3
  121.5 1.9 fusion.38
  123.9 1.4 collective-permute-start.5
  125.6 1.2 convolution_bitcast_fusion.19
  126.8 5.5 %collective-permute-done.5 = bf16[1,512,256]{2,1,0:T(8,128)(2,1)S(1)} collective-permute-done((bf16[1,512,256]{2,1,0:T(8,128)(2,1)S(1)}, bf16[1,512,256]{2,1,0:T(8,128)(2,1)S(1)}, u32[]{:S(2)}, u32[]{:S(2)}) %collective-permute-start.5) | collective-permute-done | bytes 262176 | tf_op jit(solution)/shard_map/ppermute | solution.py:13
  132.7 1.4 fusion.40
  134.5 1.3 collective-permute-start.6
  136.3 10.4 %collective-permute-done.6 = bf16[1,512,256]{2,1,0:T(8,128)(2,1)S(1)} collective-permute-done((bf16[1,512,256]{2,1,0:T(8,128)(2,1)S(1)}, bf16[1,512,256]{2,1,0:T(8,128)(2,1)S(1)}, u32[]{:S(2)}, u32[]{:S(2)}) %collective-permute-start.6) | collective-permute-done | bytes 262176 | tf_op jit(solution)/shard_map/ppermute | solution.py:13
  147.8 1.1 pad_maximum_fusion.3
  149.3 1.5 convolution_bitcast_fusion
  151.6 1.3 fusion.42
  154.1 1.5 pad_maximum_fusion.1
  155.9 1.5 convolution_bitcast_fusion.4
  157.4 1.5 convolution_bitcast_fusion.5
  158.9 1.4 convolution_bitcast_fusion.6
  160.6 1.5 pad_maximum_fusion
  164.5 5.2 %all-to-all-start = ((bf16[4,1,512,256]{3,2,1,0:T(8,128)(2,1)}), bf16[4,1,512,256]{3,2,1,0:T(8,128)(2,1)S(1)}, u32[]{:S(2)}, u32[]{:S(2)}) async-start(bf16[4,1,512,256]{3,2,1,0:T(8,128)(2,1)} %stack.82), calls=%async_computation | async-start | bytes 2097152 | tf_op jit(solution)/shard_map/all_to_all | solution.py:111
  169.7 1.4 fusion.19
  171.1 1.3 collective-permute-start.7
  172.4 16.9 %collective-permute-done.7 = bf16[1,512,256]{2,1,0:T(8,128)(2,1)S(1)} collective-permute-done((bf16[1,512,256]{2,1,0:T(8,128)(2,1)S(1)}, bf16[1,512,256]{2,1,0:T(8,128)(2,1)S(1)}, u32[]{:S(2)}, u32[]{:S(2)}) %collective-permute-start.7) | collective-permute-done | bytes 262176 | tf_op jit(solution)/shard_map/ppermute | solution.py:13
  189.3 1.3 fusion.44
  190.6 1.1 pad_maximum_fusion.2
  191.7 4.8 %all-to-all-start.1 = ((bf16[4,1,512,256]{3,2,1,0:T(8,128)(2,1)}), bf16[4,1,512,256]{3,2,1,0:T(8,128)(2,1)S(1)}, u32[]{:S(2)}, u32[]{:S(2)}) async-start(bf16[4,1,512,256]{3,2,1,0:T(8,128)(2,1)} %pad_maximum_fusion.2), calls=%async_computation.1 | async-start | bytes 2097152 | tf_op jit(solution)/shard_map/all_to_all | solution.py:140
  196.5 26.8 %reduce-scatter.7.cloned.1.call-done = f32[1,256,512]{2,1,0:T(8,128)} async-done(((f32[4,256,512]{2,1,0:T(8,128)}), f32[1,256,512]{2,1,0:T(8,128)}) %reduce-scatter.7.cloned.1.call-update) | async-done | bytes 524304 | tf_op jit(solution)/shard_map/reduce_scatter | solution.py:145
  223.3 35.1 %reduce-scatter.5.cloned.1.call-done = f32[1,256,512]{2,1,0:T(8,128)} async-done(((f32[4,256,512]{2,1,0:T(8,128)}), f32[1,256,512]{2,1,0:T(8,128)}) %reduce-scatter.5.cloned.1.call-update) | async-done | bytes 524304 | tf_op jit(solution)/shard_map/reduce_scatter | solution.py:142
  258.5 194.2 %all-reduce.3.cloned.1.call-done = (f32[1,256,512]{2,1,0:T(8,128)}, f32[1,256,512]{2,1,0:T(8,128)}, f32[1,256,256]{2,1,0:T(8,128)}, f32[1,256,256]{2,1,0:T(8,128)}) async-done(((f32[1,256,512]{2,1,0:T(8,128)}, f32[1,256,512]{2,1,0:T(8,128)}, f32[1,256,256]{2,1,0:T(8,128)}, f32[1,256,256]{2,1,0:T(8,128)}), (f32[1,256,512]{2,1,0:T(8,128)}, f32[1,256,512]{2,1,0:T(8,128)}, f32[1,256,256]{2,1,0:T(8,128)}, ...) | async-done | bytes 1572880 | tf_op jit(solution)/shard_map/psum | solution.py:166
  452.7 1.9 broadcast_multiply_fusion.2
  454.6 2.3 broadcast_multiply_fusion
  (148 shorter events, 17.5 us)
Async XLA Ops:
  7.2 39.3 %copy-start = (bf16[4,512,256]{2,1,0:T(8,128)(2,1)S(1)}, bf16[4,512,256]{2,1,0:T(8,128)(2,1)}, u32[]{:S(2)}) copy-start(bf16[4,512,256]{2,1,0:T(8,128)(2,1)} %param.8) | copy-start | bytes 3145732
  7.2 40.3 %all-gather.5.cloned.1.call-start = ((), (), s32[]{:S(2)}) async-start(), calls=%async_computation.7 | async-start | bytes 1310720 | tf_op jit(solution)/shard_map/all_gather | solution.py:87
  7.9 60.6 %all-gather.3.cloned.1.call-start = ((), (), s32[]{:S(2)}) async-start(), calls=%async_computation.6 | async-start | bytes 1310720 | tf_op jit(solution)/shard_map/all_gather | solution.py:86
  8.7 187.8 %reduce-scatter.11.cloned.1.call-start = ((), (), s32[]{:S(2)}) async-start(), calls=%async_computation.11 | async-start | bytes 1310720 | tf_op jit(solution)/shard_map/reduce_scatter | solution.py:151
  9.7 39.1 %collective-permute-start = (bf16[1,512,256]{2,1,0:T(8,128)(2,1)S(1)}, bf16[1,512,256]{2,1,0:T(8,128)(2,1)S(1)}, u32[]{:S(2)}, u32[]{:S(2)}) collective-permute-start(bf16[1,512,256]{2,1,0:T(8,128)(2,1)S(1)} %constant_dynamic-slice_fusion), channel_id=1, source_target_pairs={{0,4},{1,5},{2,6},{3,7},{4,8},{5,9},{6,10},{7,11},{8,12},{9,13},{1... | collective-permute-start | bytes 786440 | tf_op jit(solution)/shard_map/ppermute | solution.py:13
  29.1 55.0 %copy-start.11 = (bf16[4,256,256]{2,1,0:T(8,128)(2,1)}, bf16[4,256,256]{2,1,0:T(8,128)(2,1)S(1)}, u32[]{:S(2)}) copy-start(bf16[4,256,256]{2,1,0:T(8,128)(2,1)S(1)} %all_gather.15) | copy-start | bytes 1572868
  48.8 19.7 %copy-start.14 = (bf16[1,512,256]{2,1,0:T(8,128)(2,1)}, bf16[1,512,256]{2,1,0:T(8,128)(2,1)S(1)}, u32[]{:S(2)}) copy-start(bf16[1,512,256]{2,1,0:T(8,128)(2,1)S(1)} %collective-permute-done) | copy-start | bytes 786436
  69.8 8.9 %copy-start.1 = (f32[1,512,512]{1,2,0:T(8,128)}, f32[1,512,512]{1,2,0:T(8,128)S(1)}, u32[]{:S(2)}) copy-start(f32[1,512,512]{1,2,0:T(8,128)S(1)} %fusion.3) | copy-start | bytes 3145732
  69.8 8.6 %copy-start.36 = (bf16[4,256,512]{2,1,0:T(8,128)(2,1)S(1)}, bf16[4,256,512]{2,1,0:T(8,128)(2,1)}, u32[]{:S(2)}) copy-start(bf16[4,256,512]{2,1,0:T(8,128)(2,1)} %all-gather.5.cloned.1.call-done) | copy-start | bytes 3145732
  69.8 14.3 %copy-start.12 = (bf16[4,256,512]{2,1,0:T(8,128)(2,1)S(1)}, bf16[4,256,512]{2,1,0:T(8,128)(2,1)}, u32[]{:S(2)}) copy-start(bf16[4,256,512]{2,1,0:T(8,128)(2,1)} %all-gather.3.cloned.1.call-done) | copy-start | bytes 3145732
  70.5 13.6 %collective-permute-start.1 = (bf16[1,512,256]{2,1,0:T(8,128)(2,1)S(1)}, bf16[1,512,256]{2,1,0:T(8,128)(2,1)S(1)}, u32[]{:S(2)}, u32[]{:S(2)}) collective-permute-start(bf16[1,512,256]{2,1,0:T(8,128)(2,1)S(1)} %fusion.14), channel_id=1, source_target_pairs={{0,8},{1,9},{2,10},{3,11},{4,12},{5,13},{6,14},{7,15},{8,16},{9,17... | collective-permute-start | bytes 786440 | tf_op jit(solution)/shard_map/ppermute | solution.py:13
  84.5 7.1 %copy-start.3 = (f32[1,512,512]{1,2,0:T(8,128)}, f32[1,512,512]{1,2,0:T(8,128)S(1)}, u32[]{:S(2)}) copy-start(f32[1,512,512]{1,2,0:T(8,128)S(1)} %fusion.2) | copy-start | bytes 3145732
  86.3 8.8 %collective-permute-start.2 = (bf16[1,512,256]{2,1,0:T(8,128)(2,1)S(1)}, bf16[1,512,256]{2,1,0:T(8,128)(2,1)S(1)}, u32[]{:S(2)}, u32[]{:S(2)}) collective-permute-start(bf16[1,512,256]{2,1,0:T(8,128)(2,1)S(1)} %fusion.13), channel_id=1, source_target_pairs={{0,16},{1,17},{2,18},{3,19},{4,20},{5,21},{6,22},{7,23},{8,24},{9,... | collective-permute-start | bytes 786440 | tf_op jit(solution)/shard_map/ppermute | solution.py:13
  96.1 8.2 %copy-start.5 = (f32[1,512,512]{1,2,0:T(8,128)}, f32[1,512,512]{1,2,0:T(8,128)S(1)}, u32[]{:S(2)}) copy-start(f32[1,512,512]{1,2,0:T(8,128)S(1)} %fusion.1) | copy-start | bytes 3145732
  98.0 10.3 %copy-start.7 = (bf16[4,256,256]{2,1,0:T(8,128)(2,1)S(1)}, bf16[4,256,256]{2,1,0:T(8,128)(2,1)}, u32[]{:S(2)}) copy-start(bf16[4,256,256]{2,1,0:T(8,128)(2,1)} %copy-done.6) | copy-start | bytes 1572868
  98.0 10.3 %copy-start.45 = (f32[512,256]{0,1:T(8,128)S(1)}, f32[512,256]{0,1:T(8,128)}, u32[]{:S(2)}) copy-start(f32[512,256]{0,1:T(8,128)} %fusion.63) | copy-start | bytes 1572868
  98.0 9.9 %collective-permute-start.3 = (bf16[1,512,256]{2,1,0:T(8,128)(2,1)S(1)}, bf16[1,512,256]{2,1,0:T(8,128)(2,1)S(1)}, u32[]{:S(2)}, u32[]{:S(2)}) collective-permute-start(bf16[1,512,256]{2,1,0:T(8,128)(2,1)S(1)} %fusion.12), channel_id=1, source_target_pairs={{0,32},{1,33},{2,34},{3,35},{4,36},{5,37},{6,38},{7,39},{8,40},{9,... | collective-permute-start | bytes 786440 | tf_op jit(solution)/shard_map/ppermute | solution.py:13
  108.7 2.4 copy-start.8
  108.8 2.6 copy-start.20
  108.8 2.6 copy-start.21
  109.8 10.1 %collective-permute-start.4 = (bf16[1,512,256]{2,1,0:T(8,128)(2,1)}, bf16[1,512,256]{2,1,0:T(8,128)(2,1)}, u32[]{:S(2)}, u32[]{:S(2)}) collective-permute-start(bf16[1,512,256]{2,1,0:T(8,128)(2,1)} %fusion.16), channel_id=1, source_target_pairs={{32,0},{33,1},{34,2},{35,3},{36,4},{37,5},{38,6},{39,7},{40,8},{41... | collective-permute-start | bytes 786440 | tf_op jit(solution)/shard_map/ppermute | solution.py:13
  112.5 84.0 %reduce-scatter.9.cloned.1.call-start = ((), (), s32[]{:S(2)}) async-start(), calls=%async_computation.10 | async-start | bytes 1310720 | tf_op jit(solution)/shard_map/reduce_scatter | solution.py:148
  121.5 14.3 %copy-start.38 = (bf16[1,512,256]{2,1,0:T(8,128)(2,1)}, bf16[1,512,256]{2,1,0:T(8,128)(2,1)S(1)}, u32[]{:S(2)}) copy-start(bf16[1,512,256]{2,1,0:T(8,128)(2,1)S(1)} %add_convert_fusion.3) | copy-start | bytes 786436
  123.5 9.2 %copy-start.22 = (bf16[512,256]{0,1:T(8,128)(2,1)}, bf16[512,256]{0,1:T(8,128)(2,1)S(1)}, u32[]{:S(2)}) copy-start(bf16[512,256]{0,1:T(8,128)(2,1)S(1)} %get-tuple-element.14) | copy-start | bytes 786436
  123.5 9.2 %copy-start.24 = (bf16[512,256]{0,1:T(8,128)(2,1)}, bf16[512,256]{0,1:T(8,128)(2,1)S(1)}, u32[]{:S(2)}) copy-start(bf16[512,256]{0,1:T(8,128)(2,1)S(1)} %get-tuple-element.15) | copy-start | bytes 786436
  123.5 8.8 %copy-start.37 = (bf16[4,256,512]{2,1,0:T(8,128)(2,1)S(1)}, bf16[4,256,512]{2,1,0:T(8,128)(2,1)}, u32[]{:S(2)}) copy-start(bf16[4,256,512]{2,1,0:T(8,128)(2,1)} %all-gather.5.cloned.1.call-done) | copy-start | bytes 3145732
  123.9 8.8 %copy-start.4 = (f32[1,512,512]{1,2,0:T(8,128)S(1)}, f32[1,512,512]{1,2,0:T(8,128)}, u32[]{:S(2)}) copy-start(f32[1,512,512]{1,2,0:T(8,128)} %copy-done.3) | copy-start | bytes 3145732
  123.9 8.4 %collective-permute-start.5 = (bf16[1,512,256]{2,1,0:T(8,128)(2,1)S(1)}, bf16[1,512,256]{2,1,0:T(8,128)(2,1)S(1)}, u32[]{:S(2)}, u32[]{:S(2)}) collective-permute-start(bf16[1,512,256]{2,1,0:T(8,128)(2,1)S(1)} %fusion.17), channel_id=1, source_target_pairs={{16,0},{17,1},{18,2},{19,3},{20,4},{21,5},{22,6},{23,7},{24,8},{25... | collective-permute-start | bytes 786440 | tf_op jit(solution)/shard_map/ppermute | solution.py:13
  132.7 14.0 %copy-start.40 = (bf16[1,512,256]{2,1,0:T(8,128)(2,1)}, bf16[1,512,256]{2,1,0:T(8,128)(2,1)S(1)}, u32[]{:S(2)}) copy-start(bf16[1,512,256]{2,1,0:T(8,128)(2,1)S(1)} %add_convert_fusion.2) | copy-start | bytes 786436
  134.1 12.9 %copy-start.32 = (bf16[512,256]{0,1:T(8,128)(2,1)}, bf16[512,256]{0,1:T(8,128)(2,1)S(1)}, u32[]{:S(2)}) copy-start(bf16[512,256]{0,1:T(8,128)(2,1)S(1)} %get-tuple-element.12) | copy-start | bytes 786436
  134.1 12.9 %copy-start.34 = (bf16[512,256]{0,1:T(8,128)(2,1)}, bf16[512,256]{0,1:T(8,128)(2,1)S(1)}, u32[]{:S(2)}) copy-start(bf16[512,256]{0,1:T(8,128)(2,1)S(1)} %get-tuple-element.13) | copy-start | bytes 786436
  134.5 12.2 %collective-permute-start.6 = (bf16[1,512,256]{2,1,0:T(8,128)(2,1)S(1)}, bf16[1,512,256]{2,1,0:T(8,128)(2,1)S(1)}, u32[]{:S(2)}, u32[]{:S(2)}) collective-permute-start(bf16[1,512,256]{2,1,0:T(8,128)(2,1)S(1)} %fusion.18), channel_id=1, source_target_pairs={{8,0},{9,1},{10,2},{11,3},{12,4},{13,5},{14,6},{15,7},{16,8},{17,9... | collective-permute-start | bytes 786440 | tf_op jit(solution)/shard_map/ppermute | solution.py:13
  149.0 74.4 %reduce-scatter.7.cloned.1.call-start = ((), (), s32[]{:S(2)}) async-start(), calls=%async_computation.9 | async-start | bytes 2621440 | tf_op jit(solution)/shard_map/reduce_scatter | solution.py:145
  149.3 2.3 copy-start.2
  155.6 3.3 copy-start.17
  155.6 4.6 copy-start.15
  155.6 102.8 %reduce-scatter.5.cloned.1.call-start = ((), (), s32[]{:S(2)}) async-start(), calls=%async_computation.8 | async-start | bytes 2621440 | tf_op jit(solution)/shard_map/reduce_scatter | solution.py:142
  155.9 4.4 copy-start.27
  155.9 4.4 copy-start.30
  163.2 6.5 %copy-start.28 = (bf16[512,256]{0,1:T(8,128)(2,1)S(1)}, bf16[512,256]{0,1:T(8,128)(2,1)}, u32[]{:S(2)}) copy-start(bf16[512,256]{0,1:T(8,128)(2,1)} %copy-done.26) | copy-start | bytes 786436
  163.4 6.3 %copy-start.31 = (bf16[512,256]{0,1:T(8,128)(2,1)S(1)}, bf16[512,256]{0,1:T(8,128)(2,1)}, u32[]{:S(2)}) copy-start(bf16[512,256]{0,1:T(8,128)(2,1)} %copy-done.29) | copy-start | bytes 786436
  164.5 24.8 %copy-start.44 = (bf16[1,512,256]{2,1,0:T(8,128)(2,1)S(1)}, bf16[1,512,256]{2,1,0:T(8,128)(2,1)}, u32[]{:S(2)}) copy-start(bf16[1,512,256]{2,1,0:T(8,128)(2,1)} %copy-done.42) | copy-start | bytes 786436
  164.5 27.2 %all-to-all-start = ((bf16[4,1,512,256]{3,2,1,0:T(8,128)(2,1)}), bf16[4,1,512,256]{3,2,1,0:T(8,128)(2,1)S(1)}, u32[]{:S(2)}, u32[]{:S(2)}) async-start(bf16[4,1,512,256]{3,2,1,0:T(8,128)(2,1)} %stack.82), calls=%async_computation | async-start | bytes 2097152 | tf_op jit(solution)/shard_map/all_to_all | solution.py:111
  169.7 20.9 %copy-start.39 = (bf16[1,512,256]{2,1,0:T(8,128)(2,1)S(1)}, bf16[1,512,256]{2,1,0:T(8,128)(2,1)}, u32[]{:S(2)}) copy-start(bf16[1,512,256]{2,1,0:T(8,128)(2,1)} %copy-done.38) | copy-start | bytes 786436
  169.7 20.9 %copy-start.41 = (bf16[1,512,256]{2,1,0:T(8,128)(2,1)S(1)}, bf16[1,512,256]{2,1,0:T(8,128)(2,1)}, u32[]{:S(2)}) copy-start(bf16[1,512,256]{2,1,0:T(8,128)(2,1)} %copy-done.40) | copy-start | bytes 786436
  171.1 18.2 %collective-permute-start.7 = (bf16[1,512,256]{2,1,0:T(8,128)(2,1)S(1)}, bf16[1,512,256]{2,1,0:T(8,128)(2,1)S(1)}, u32[]{:S(2)}, u32[]{:S(2)}) collective-permute-start(bf16[1,512,256]{2,1,0:T(8,128)(2,1)S(1)} %fusion.19), channel_id=1, source_target_pairs={{4,0},{5,1},{6,2},{7,3},{8,4},{9,5},{10,6},{11,7},{12,8},{13,9},{1... | collective-permute-start | bytes 786440 | tf_op jit(solution)/shard_map/ppermute | solution.py:13
  191.7 66.8 %all-to-all-start.1 = ((bf16[4,1,512,256]{3,2,1,0:T(8,128)(2,1)}), bf16[4,1,512,256]{3,2,1,0:T(8,128)(2,1)S(1)}, u32[]{:S(2)}, u32[]{:S(2)}) async-start(bf16[4,1,512,256]{3,2,1,0:T(8,128)(2,1)} %pad_maximum_fusion.2), calls=%async_computation.1 | async-start | bytes 2097152 | tf_op jit(solution)/shard_map/all_to_all | solution.py:140
  196.5 256.2 %all-reduce.3.cloned.1.call-start = ((), (), s32[]{:S(2)}) async-start(), calls=%async_computation.12 | async-start | bytes 3145728 | tf_op jit(solution)/shard_map/psum | solution.py:166
  (15 other events, 23.1 us)
Sparse Core Ops, SparseCore 0:
  9.8 30.3 all-gather.4
  42.0 26.4 all-gather.2
  112.6 31.7 reduce-scatter.10
  149.1 34.1 reduce-scatter.8
  185.7 37.6 reduce-scatter.6
  225.7 32.7 reduce-scatter.4
  262.1 190.5 all-reduce.2
